TPU v7x, 32 devices: a whole 2x2x4 slice. The times are simulated.
32 devices in a mesh: row: 8 (over y, x, core), col: 4 (over z).
Axes of the slice: x: 2, y: 2, z: 4, core: 2. Of those that a mesh axis runs over, the one named last changes fastest.
Arguments:
- block_input: bfloat16 [8192, 768], P(('row', 'col'))
- block_cotangent: bfloat16 [8192, 768], P(('row', 'col')), may hold values from -6 to 6
- block_lengths: int32 [64], P(('row', 'col')), may hold values from 1 to 128, as said below
- block_offsets: int32 [64], P(('row', 'col')), may hold values from 0 to 128, as said below
- norm1_gain: float32 [768], replicated, may hold values from 0.25 to 1.75
- norm1_bias: float32 [768], replicated, may hold values from -2.5 to 2.5
- norm2_gain: float32 [768], replicated, may hold values from 0.25 to 1.75
- norm2_bias: float32 [768], replicated, may hold values from -2.5 to 2.5
- qkv_weight: bfloat16 [768, 2304], P('row', 'col'), may hold values from -0.21875 to 0.21875
- qkv_bias: float32 [2304], P('col'), may hold values from -3 to 3
- dense_weight: bfloat16 [768, 768], P('col', 'row'), may hold values from -0.875 to 0.875
- dense_bias: float32 [768], replicated, may hold values from -2.5 to 2.5
- fc_in_weight: bfloat16 [768, 3072], P('row', 'col'), may hold values from -0.21875 to 0.21875
- fc_in_bias: float32 [3072], P('col'), may hold values from -3 to 3
- fc_out_weight: bfloat16 [3072, 768], P('col', 'row'), may hold values from -0.109375 to 0.109375
- fc_out_bias: float32 [768], replicated, may hold values from -2.5 to 2.5
Outputs:
- block_out: float32 [8192, 768], P(('row', 'col'))
- input_grad: float32 [8192, 768], P(('row', 'col'))
- norm1_gain_grad: float32 [768], replicated
- norm1_bias_grad: float32 [768], replicated
- norm2_gain_grad: float32 [768], replicated
- norm2_bias_grad: float32 [768], replicated
- qkv_weight_grad: float32 [768, 2304], P('row', 'col')
- qkv_bias_grad: float32 [2304], P('col')
- dense_weight_grad: float32 [768, 768], P('col', 'row')
- dense_bias_grad: float32 [768], replicated
- fc_in_weight_grad: float32 [768, 3072], P('row', 'col')
- fc_in_bias_grad: float32 [3072], P('col')
- fc_out_weight_grad: float32 [3072, 768], P('col', 'row')
- fc_out_bias_grad: float32 [768], replicated
Inputs may be any that keep to these rules, and one draw needn't show every extreme that they name: `block_lengths`: blocks come in aligned pairs. A pair holds either two sequences, each in its own block, or one sequence over both blocks, whose first block is then full. `block_offsets`: an even block's offset is 0; an odd block's is 0 when it starts a sequence and 128 when it continues the sequence of the block before it.
All inputs are finite; a program needn't handle non-finite values.
Results may differ from a plain program's by a relative error of at most 0.0088.
Values may be sent and summed in bfloat16 or wider, within the bound.
A program may use at most 128 MiB of HBM per device.

v0:
```python
import math
import jax
import jax.numpy as jnp
from jax import lax
from jax.sharding import PartitionSpec as P

HEADS = 12
ROT = 16
NORM_EPSILON = 1e-05
HALF_ROOT = math.sqrt(0.5)
DENSITY_SCALE = 1.0 / math.sqrt(2.0 * math.pi)


def normalize(features):
    widened = features.astype(jnp.float32)
    centered = widened - jnp.mean(widened, axis=1, keepdims=True)
    inverse = lax.rsqrt(jnp.mean(centered * centered, axis=1, keepdims=True) + NORM_EPSILON)
    return (centered * inverse, inverse)


def norm_back(grad_normed, gain, standard, inverse):
    grad_unit = grad_normed * gain
    return inverse * (
        grad_unit
        - jnp.mean(grad_unit, axis=1, keepdims=True)
        - standard * jnp.mean(grad_unit * standard, axis=1, keepdims=True)
    )


def gelu_exact(pre_act):
    return 0.5 * pre_act * (1.0 + lax.erf(pre_act * HALF_ROOT))


def gelu_slope(pre_act):
    return (
        0.5 * (1.0 + lax.erf(pre_act * HALF_ROOT))
        + pre_act * jnp.exp(-0.5 * pre_act * pre_act) * DENSITY_SCALE
    )


def rotary_tables(positions, rotated):
    halves = rotated // 2
    frequency = 10000.0 ** (-2.0 * jnp.arange(halves, dtype=jnp.float32) / rotated)
    angles = positions[:, None].astype(jnp.float32) * frequency[None, :]
    angles = jnp.concatenate([angles, angles], axis=1)
    return (jnp.cos(angles)[:, None, :], jnp.sin(angles)[:, None, :])


def rotate(values, cosine, sine_table, rotated):
    halves = rotated // 2
    leading = values[..., :rotated]
    turned = jnp.concatenate([-leading[..., halves:], leading[..., :halves]], axis=-1)
    return jnp.concatenate([leading * cosine + turned * sine_table, values[..., rotated:]], axis=-1)


def unrotate(gradient, cosine, sine_table, rotated):
    halves = rotated // 2
    leading = gradient[..., :rotated]
    scaled = leading * sine_table
    turned = jnp.concatenate([scaled[..., halves:], -scaled[..., :halves]], axis=-1)
    return jnp.concatenate([leading * cosine + turned, gradient[..., rotated:]], axis=-1)


def pair_mask(lengths, offsets, block_rows):
    pair_count = lengths.shape[0] // 2
    local_rows = jnp.arange(2 * block_rows, dtype=jnp.int32)
    block_of = local_rows // block_rows
    in_block = local_rows % block_rows
    pair_lengths = lengths.reshape(pair_count, 2)
    joined = offsets.reshape(pair_count, 2)[:, 1] > 0
    row_limit = jnp.where(block_of[None, :] == 0, pair_lengths[:, 0:1], pair_lengths[:, 1:2])
    live_keys = in_block[None, :] < row_limit
    same_seq = (block_of[:, None] == block_of[None, :])[None, :, :] | joined[:, None, None]
    causal = (local_rows[None, :] <= local_rows[:, None])[None, :, :]
    diagonal = (local_rows[:, None] == local_rows[None, :])[None, :, :]
    return same_seq & causal & (live_keys[:, None, :] | diagonal)


def masked_scores(queries, key_rows, allowed, score_scale):
    scores = (
        jnp.einsum("pihd,pjhd->phij", queries, key_rows, preferred_element_type=jnp.float32)
        * score_scale
    )
    return jnp.where(allowed[:, None, :, :], scores, -jnp.inf)


def on_device(
    block_input,
    block_cotangent,
    block_lengths,
    block_offsets,
    norm1_gain,
    norm1_bias,
    norm2_gain,
    norm2_bias,
    qkv_weight,
    qkv_bias,
    dense_weight,
    dense_bias,
    fc_in_weight,
    fc_in_bias,
    fc_out_weight,
    fc_out_bias,
):
    groups = lax.axis_size("col")
    col_index = lax.axis_index("col")
    own_rows = block_input.shape[0]
    width = block_input.shape[1]
    head_dim = width // HEADS
    block_count = block_lengths.shape[0]
    block_rows = own_rows // block_count
    pair_count = block_count // 2
    four_shape = (pair_count, 2 * block_rows, HEADS, head_dim)
    score_scale = head_dim ** (-0.5)
    contract_rows = (((0,), (0,)), ((), ()))
    in_block = jnp.arange(block_rows, dtype=jnp.int32)
    positions = (block_offsets[:, None] + in_block[None, :]).reshape(-1)
    valid = (in_block[None, :] < block_lengths[:, None]).reshape(-1)
    cosine, sine_table = rotary_tables(positions, ROT)
    allowed = pair_mask(block_lengths, block_offsets, block_rows)
    standard, inverse = normalize(block_input)
    normed_first = (standard * norm1_gain + norm1_bias).astype(jnp.bfloat16)
    normed_second = (standard * norm2_gain + norm2_bias).astype(jnp.bfloat16)
    first_rows, second_rows = (
        lax.all_gather(normed_first, "col", axis=0, tiled=True),
        lax.all_gather(normed_second, "col", axis=0, tiled=True),
    )
    qkv_block, fc_in_block, dense_block, fc_out_block = (
        lax.all_gather(qkv_weight, "row", axis=0, tiled=True),
        lax.all_gather(fc_in_weight, "row", axis=0, tiled=True),
        lax.all_gather(dense_weight, "row", axis=1, tiled=True),
        lax.all_gather(fc_out_weight, "row", axis=1, tiled=True),
    )
    mixed_rows = (
        jnp.dot(first_rows, qkv_block, preferred_element_type=jnp.float32) + qkv_bias
    ).astype(jnp.bfloat16)
    mixed_own = lax.all_to_all(mixed_rows, "col", split_axis=0, concat_axis=1, tiled=True)
    mixed_own = mixed_own.reshape(own_rows, 3, HEADS, head_dim)
    queries = rotate(mixed_own[:, 0].astype(jnp.float32), cosine, sine_table, ROT).astype(
        jnp.bfloat16
    )
    key_rows = rotate(mixed_own[:, 1].astype(jnp.float32), cosine, sine_table, ROT).astype(
        jnp.bfloat16
    )
    queries = queries.reshape(four_shape)
    key_rows = key_rows.reshape(four_shape)
    values = mixed_own[:, 2].reshape(four_shape)
    scores = masked_scores(queries, key_rows, allowed, score_scale)
    highest = jnp.max(scores, axis=-1, keepdims=True)
    totals = highest + jnp.log(jnp.sum(jnp.exp(scores - highest), axis=-1, keepdims=True))
    weights = jnp.exp(scores - totals).astype(jnp.bfloat16)
    attended = jnp.einsum("phij,pjhd->pihd", weights, values, preferred_element_type=jnp.float32)
    attended = attended.astype(jnp.bfloat16).reshape(own_rows, width)
    attended_rows = lax.all_to_all(attended, "col", split_axis=1, concat_axis=0, tiled=True)
    pre_act = jnp.dot(second_rows, fc_in_block, preferred_element_type=jnp.float32) + fc_in_bias
    hidden = gelu_exact(pre_act).astype(jnp.bfloat16)
    summed = lax.psum_scatter(
        (
            jnp.dot(attended_rows, dense_block, preferred_element_type=jnp.float32)
            + jnp.dot(hidden, fc_out_block, preferred_element_type=jnp.float32)
        ).astype(jnp.bfloat16),
        "col",
        scatter_dimension=0,
        tiled=True,
    ).astype(jnp.float32)
    block_out = block_input.astype(jnp.float32) + dense_bias + fc_out_bias + summed
    grad_out = jnp.where(valid[:, None], block_cotangent, jnp.zeros_like(block_cotangent))
    grad_rows = lax.all_gather(grad_out, "col", axis=0, tiled=True)
    grad_hidden = jnp.dot(grad_rows, fc_out_block.T, preferred_element_type=jnp.float32)
    grad_pre = (grad_hidden * gelu_slope(pre_act)).astype(jnp.bfloat16)
    grad_att_rows = jnp.dot(grad_rows, dense_block.T, preferred_element_type=jnp.float32).astype(
        jnp.bfloat16
    )
    grad_att = lax.all_to_all(
        grad_att_rows, "col", split_axis=0, concat_axis=1, tiled=True
    ).reshape(four_shape)
    probability = jnp.exp(scores - totals)
    grad_probs = jnp.einsum("pihd,pjhd->phij", grad_att, values, preferred_element_type=jnp.float32)
    row_dot = jnp.sum(probability * grad_probs, axis=-1, keepdims=True)
    grad_scores = (probability * (grad_probs - row_dot) * score_scale).astype(jnp.bfloat16)
    grad_query = jnp.einsum(
        "phij,pjhd->pihd", grad_scores, key_rows, preferred_element_type=jnp.float32
    )
    grad_key = jnp.einsum(
        "phij,pihd->pjhd", grad_scores, queries, preferred_element_type=jnp.float32
    )
    grad_values = jnp.einsum(
        "phij,pihd->pjhd", weights, grad_att, preferred_element_type=jnp.float32
    )
    grad_query = unrotate(
        grad_query.reshape(own_rows, HEADS, head_dim), cosine, sine_table, ROT
    ).astype(jnp.bfloat16)
    grad_key = unrotate(
        grad_key.reshape(own_rows, HEADS, head_dim), cosine, sine_table, ROT
    ).astype(jnp.bfloat16)
    grad_values = grad_values.astype(jnp.bfloat16).reshape(own_rows, HEADS, head_dim)
    grad_mixed = jnp.stack([grad_query, grad_key, grad_values], axis=1).reshape(own_rows, 3 * width)
    grad_mixed_rows = lax.all_to_all(grad_mixed, "col", split_axis=1, concat_axis=0, tiled=True)
    grad_qkv_w = lax.dot_general(
        first_rows, grad_mixed_rows, contract_rows, preferred_element_type=jnp.float32
    )
    grad_in_w = lax.dot_general(
        second_rows, grad_pre, contract_rows, preferred_element_type=jnp.float32
    )
    qkv_weight_grad, fc_in_weight_grad = (
        lax.psum_scatter(grad_qkv_w, "row", scatter_dimension=0, tiled=True),
        lax.psum_scatter(grad_in_w, "row", scatter_dimension=0, tiled=True),
    )
    grad_dense_w = lax.dot_general(
        attended_rows, grad_rows, contract_rows, preferred_element_type=jnp.float32
    )
    grad_out_w = lax.dot_general(
        hidden, grad_rows, contract_rows, preferred_element_type=jnp.float32
    )
    dense_weight_grad, fc_out_weight_grad = (
        lax.psum_scatter(grad_dense_w, "row", scatter_dimension=1, tiled=True),
        lax.psum_scatter(grad_out_w, "row", scatter_dimension=1, tiled=True),
    )
    back_first_rows = jnp.dot(grad_mixed_rows, qkv_block.T, preferred_element_type=jnp.float32)
    back_second_rows = jnp.dot(grad_pre, fc_in_block.T, preferred_element_type=jnp.float32)
    back_first, back_second = (
        lax.psum_scatter(back_first_rows, "col", scatter_dimension=0, tiled=True),
        lax.psum_scatter(back_second_rows, "col", scatter_dimension=0, tiled=True),
    )
    input_grad = (
        grad_out.astype(jnp.float32)
        + norm_back(back_first, norm1_gain, standard, inverse)
        + norm_back(back_second, norm2_gain, standard, inverse)
    )
    norm_sums = (
        jnp.sum(back_first * standard, axis=0),
        jnp.sum(back_first, axis=0),
        jnp.sum(back_second * standard, axis=0),
        jnp.sum(back_second, axis=0),
    )
    qkv_cols = grad_mixed_rows.shape[1]
    ff_cols = grad_pre.shape[1]
    column_mask = (jnp.arange(groups, dtype=jnp.int32) == col_index)[:, None]
    qkv_bias_part = jnp.sum(grad_mixed_rows, axis=0, dtype=jnp.float32)
    in_bias_part = jnp.sum(grad_pre, axis=0, dtype=jnp.float32)
    spread_qkv = jnp.where(column_mask, qkv_bias_part[None, :], 0.0).reshape(-1)
    spread_in = jnp.where(column_mask, in_bias_part[None, :], 0.0).reshape(-1)
    gain_one, bias_one, gain_two, bias_two, out_bias, total_qkv, total_in = lax.psum(
        (
            norm_sums[0],
            norm_sums[1],
            norm_sums[2],
            norm_sums[3],
            jnp.sum(grad_out, axis=0, dtype=jnp.float32),
            spread_qkv,
            spread_in,
        ),
        ("row", "col"),
    )
    qkv_bias_grad = lax.dynamic_slice_in_dim(total_qkv, col_index * qkv_cols, qkv_cols, 0)
    fc_in_bias_grad = lax.dynamic_slice_in_dim(total_in, col_index * ff_cols, ff_cols, 0)
    return (
        block_out,
        input_grad,
        gain_one,
        bias_one,
        gain_two,
        bias_two,
        qkv_weight_grad,
        qkv_bias_grad,
        dense_weight_grad,
        out_bias,
        fc_in_weight_grad,
        fc_in_bias_grad,
        fc_out_weight_grad,
        out_bias,
    )


def solution(mesh):
    return jax.shard_map(
        on_device,
        mesh=mesh,
        in_specs=(
            P(("row", "col"), None),
            P(("row", "col"), None),
            P(("row", "col")),
            P(("row", "col")),
            P(),
            P(),
            P(),
            P(),
            P("row", "col"),
            P("col"),
            P("col", "row"),
            P(),
            P("row", "col"),
            P("col"),
            P("col", "row"),
            P(),
        ),
        out_specs=(
            P(("row", "col"), None),
            P(("row", "col"), None),
            P(),
            P(),
            P(),
            P(),
            P("row", "col"),
            P("col"),
            P("col", "row"),
            P(),
            P("row", "col"),
            P("col"),
            P("col", "row"),
            P(),
        ),
        check_vma=False,
    )
```

profile of v0, /device:TPU:0, one launch (start us, length us, event | category | flops | bytes accessed | tf_op | source)
XLA Modules:
  0.0 555.2 jit_solution(1927547153196983552)
XLA Ops:
  9.7 2.2 fusion.38
  15.7 12.3 %all_gather.22 = bf16[768,576]{1,0:T(8,128)(2,1)S(1)} all-gather(bf16[96,576]{1,0:T(8,128)(2,1)S(1)} %copy-done.18), channel_id=1, replica_groups=mesh['row'=8,'col'=4] {'row'}, dimensions={0}, use_global_device_ids=true | all-gather | bytes 995328 | tf_op jit(solution)/shard_map/all_gather | solution.py:129
  28.0 23.8 %all-gather.6.cloned.1.call-done = bf16[1024,768]{1,0:T(8,128)(2,1)} async-done(((bf16[256,768]{1,0:T(8,128)(2,1)}), bf16[1024,768]{1,0:T(8,128)(2,1)}) %all-gather.6.cloned.1.call-update) | async-done | bytes 1572880 | tf_op jit(solution)/shard_map/all_gather | solution.py:125
  51.8 2.5 add_convert_fusion.1
  55.5 3.5 all-to-all-start
  63.2 23.8 %all-to-all-done = bf16[4,256,576]{1,2,0:T(8,128)(2,1)S(1)} async-done(((bf16[4,256,576]{1,2,0:T(8,128)(2,1)}), bf16[4,256,576]{1,2,0:T(8,128)(2,1)S(1)}, u32[]{:S(2)}, u32[]{:S(2)}) %all-to-all-start) | async-done | bytes 1179680 | tf_op jit(solution)/shard_map/all_to_all | solution.py:137
  91.2 3.5 all-to-all-start.1
  94.7 29.5 %all-gather.8.cloned.1.call-done = bf16[1024,768]{1,0:T(8,128)(2,1)} async-done(((bf16[256,768]{1,0:T(8,128)(2,1)}), bf16[1024,768]{1,0:T(8,128)(2,1)}) %all-gather.8.cloned.1.call-update) | async-done | bytes 1572880 | tf_op jit(solution)/shard_map/all_gather | solution.py:126
  124.2 5.4 multiply_convert_fusion.1
  129.6 31.8 %all-gather.14.cloned.1.call-done = bf16[1024,768]{1,0:T(8,128)(2,1)} async-done(((bf16[256,768]{1,0:T(8,128)(2,1)}), bf16[1024,768]{1,0:T(8,128)(2,1)}) %all-gather.14.cloned.1.call-update) | async-done | bytes 1572880 | tf_op jit(solution)/shard_map/all_gather | solution.py:168
  161.4 3.1 convolution_bitcast_fusion
  164.6 21.3 %all-gather.12.cloned.1.call-done = bf16[768,768]{0,1:T(8,128)(2,1)} async-done(((bf16[768,96]{0,1:T(8,128)(2,1)}), bf16[768,768]{0,1:T(8,128)(2,1)}) %all-gather.12.cloned.1.call-update) | async-done | bytes 1179664 | tf_op jit(solution)/shard_map/all_gather | solution.py:132
  186.0 4.7 convert_reduce_fusion
  191.9 3.1 fusion.99
  196.5 9.5 %all_gather.23 = bf16[192,768]{0,1:T(8,128)(2,1)S(1)} all-gather(bf16[192,96]{0,1:T(8,128)(2,1)} %copy.47), channel_id=1, replica_groups=mesh['row'=8,'col'=4] {'row'}, dimensions={1}, use_global_device_ids=true | all-gather | bytes 331776 | tf_op jit(solution)/shard_map/all_gather | solution.py:131
  206.7 16.6 %all_to_all.70 = bf16[4,256,192]{1,2,0:T(8,128)(2,1)S(1)} all-to-all(bf16[4,256,192]{1,2,0:T(8,128)(2,1)S(1)} %bitcast.111), channel_id=1, replica_groups=mesh['row'=8,'col'=4] {'col'}, dimensions={0} | all-to-all | bytes 786432 | tf_op jit(solution)/shard_map/all_to_all | solution.py:174
  224.1 2.3 fusion.53
  226.4 7.0 %fusion.19 = f32[256,12,64]{0,2,1:T(8,128)S(1)} fusion(f32[12,256,256]{1,2,0:T(8,128)} %fusion.53, f32[12,256,256]{1,2,0:T(8,128)} %copy-done.3, f32[12,256]{1,0:T(8,128)} %copy-done.29, pred[256,256]{0,1:T(8,128)(4,1)} %copy-done.14, bf16[256,12,48]{0,2,1:T(8,128)(2,1)} %copy-done.11, bf16[256,12,16]{0,2,1:T(8,128)(2,1)} %copy-done.20), kind=kOutput, calls=%fused_computation.25 | convolution fusion | flops 110103808 | bytes 7548928 | tf_op jit(solution)/shard_map/phij,pjhd->pihd/dot_general | solution.py:181
  233.4 7.8 %fusion.22 = f32[256,12,64]{0,2,1:T(8,128)} fusion(f32[12,256,256]{1,2,0:T(8,128)} %fusion.53, f32[12,256,256]{1,2,0:T(8,128)} %copy-done.3, f32[12,256]{1,0:T(8,128)S(1)} %copy-done.30, pred[256,256]{0,1:T(8,128)(4,1)} %copy-done.14, bf16[256,12,48]{0,2,1:T(8,128)(2,1)S(1)} %copy-done.13, bf16[256,12,16]{0,2,1:T(8,128)(2,1)} %copy-done.19), kind=kOutput, calls=%fused_computation.26 | convolution fusion | flops 110103808 | bytes 7548928 | tf_op jit(solution)/shard_map/phij,pihd->pjhd/dot_general | solution.py:184
  245.6 61.8 %all_to_all.71 = bf16[256,4,576]{0,2,1:T(8,128)(2,1)S(1)} all-to-all(bf16[256,4,576]{0,2,1:T(8,128)(2,1)S(1)} %bitcast.104), channel_id=1, replica_groups=mesh['row'=8,'col'=4] {'col'}, dimensions={1} | all-to-all | bytes 2359296 | tf_op jit(solution)/shard_map/all_to_all | solution.py:198
  308.6 3.2 fusion.98
  311.8 3.2 fusion.97
  316.9 4.8 fusion.101
  321.7 4.3 fusion.102
  326.4 4.6 fusion.100
  333.4 40.4 %reduce-scatter.12.cloned.1.call-done = f32[256,768]{1,0:T(8,128)} async-done(((f32[1024,768]{1,0:T(8,128)}), f32[256,768]{1,0:T(8,128)}) %reduce-scatter.12.cloned.1.call-update) | async-done | bytes 786448 | tf_op jit(solution)/shard_map/reduce_scatter | solution.py:222
  373.8 2.1 fusion.48
  375.8 43.6 %all-reduce = (f32[768]{0:T(1024)}, f32[768]{0:T(1024)}, f32[768]{0:T(1024)}, f32[768]{0:T(1024)}, f32[2304]{0:T(1024)S(1)}, /*index=5*/f32[768]{0:T(1024)S(1)}, f32[3072]{0:T(1024)S(1)}) all-reduce(f32[768]{0:T(1024)S(1)} %get-tuple-element.16, f32[768]{0:T(1024)S(1)} %get-tuple-element.21, ...), channel_id=1, replica_groups=mesh['row'=8,'col'=4] {'row','col'}, use_global_device_ids=true, to_apply=%region_13.14 | all-reduce | flops 9216 | bytes 73728 | tf_op jit(solution)/shard_map/psum | solution.py:243
  420.9 3.2 fusion.47
  424.1 33.4 %reduce-scatter.18.cloned.1.call-done = f32[96,768]{1,0:T(8,128)} async-done(((f32[768,768]{1,0:T(8,128)}), f32[96,768]{1,0:T(8,128)}) %reduce-scatter.18.cloned.1.call-update) | async-done | bytes 294928 | tf_op jit(solution)/shard_map/reduce_scatter | solution.py:207
  457.5 46.3 %reduce-scatter.20.cloned.1.call-done = f32[768,96]{0,1:T(8,128)} async-done(((f32[768,768]{0,1:T(8,128)}), f32[768,96]{0,1:T(8,128)}) %reduce-scatter.20.cloned.1.call-update) | async-done | bytes 294928 | tf_op jit(solution)/shard_map/reduce_scatter | solution.py:217
  503.8 44.0 %reduce-scatter.16.cloned.1.call-done = f32[96,576]{1,0:T(8,128)} async-done(((f32[768,576]{1,0:T(8,128)}), f32[96,576]{1,0:T(8,128)}) %reduce-scatter.16.cloned.1.call-update) | async-done | bytes 221200 | tf_op jit(solution)/shard_map/reduce_scatter | solution.py:206
  (166 shorter events, 31.1 us)
Async XLA Ops:
  7.2 8.5 %copy-start.18 = (bf16[96,576]{1,0:T(8,128)(2,1)S(1)}, bf16[96,576]{1,0:T(8,128)(2,1)}, u32[]{:S(2)}) copy-start(bf16[96,576]{1,0:T(8,128)(2,1)} %param.24) | copy-start | bytes 331780
  7.2 44.6 %copy-start.38 = (f32[576]{0:T(1024)S(1)}, f32[576]{0:T(1024)}, u32[]{:S(2)}) copy-start(f32[576]{0:T(1024)} %param.25) | copy-start | bytes 6916
  7.2 44.6 %all-gather.6.cloned.1.call-start = ((), (), s32[]{:S(2)}) async-start(), calls=%async_computation.11 | async-start | bytes 1966080 | tf_op jit(solution)/shard_map/all_gather | solution.py:125
  11.9 82.8 %all-gather.10.cloned.1.call-start = ((), (), s32[]{:S(2)}) async-start(), calls=%async_computation.13 | async-start | bytes 1327104 | tf_op jit(solution)/shard_map/all_gather | solution.py:130
  12.7 111.5 %all-gather.8.cloned.1.call-start = ((), (), s32[]{:S(2)}) async-start(), calls=%async_computation.12 | async-start | bytes 1966080 | tf_op jit(solution)/shard_map/all_gather | solution.py:126
  13.4 148.0 %all-gather.14.cloned.1.call-start = ((), (), s32[]{:S(2)}) async-start(), calls=%async_computation.16 | async-start | bytes 1966080 | tf_op jit(solution)/shard_map/all_gather | solution.py:168
  28.0 26.4 %copy-start.8 = (bf16[768,576]{1,0:T(8,128)(2,1)}, bf16[768,576]{1,0:T(8,128)(2,1)S(1)}, u32[]{:S(2)}) copy-start(bf16[768,576]{1,0:T(8,128)(2,1)S(1)} %all_gather.22) | copy-start | bytes 2654212
  55.5 31.4 %all-to-all-start = ((bf16[4,256,576]{1,2,0:T(8,128)(2,1)}), bf16[4,256,576]{1,2,0:T(8,128)(2,1)S(1)}, u32[]{:S(2)}, u32[]{:S(2)}) async-start(bf16[4,256,576]{1,2,0:T(8,128)(2,1)} %bitcast.101), calls=%async_computation | async-start | bytes 2359296 | tf_op jit(solution)/shard_map/all_to_all | solution.py:137
  59.1 126.9 %all-gather.12.cloned.1.call-start = ((), (), s32[]{:S(2)}) async-start(), calls=%async_computation.14 | async-start | bytes 1327104 | tf_op jit(solution)/shard_map/all_gather | solution.py:132
  63.0 25.8 %copy-start.16 = (f32[256,16]{0,1:T(8,128)}, f32[256,16]{0,1:T(8,128)S(1)}, u32[]{:S(2)}) copy-start(f32[256,16]{0,1:T(8,128)S(1)} %get-tuple-element.58) | copy-start | bytes 49156
  63.2 26.4 %copy-start.14 = (pred[256,256]{0,1:T(8,128)(4,1)}, pred[256,256]{0,1:T(8,128)(4,1)S(1)}, u32[]{:S(2)}) copy-start(pred[256,256]{0,1:T(8,128)(4,1)S(1)} %fusion.57) | copy-start | bytes 196612
  89.5 34.7 %copy-start.39 = (f32[768]{0:T(1024)S(1)}, f32[768]{0:T(1024)}, u32[]{:S(2)}) copy-start(f32[768]{0:T(1024)} %param.29) | copy-start | bytes 9220
  91.2 38.4 %all-to-all-start.1 = ((bf16[256,4,192]{0,2,1:T(8,128)(2,1)}), bf16[256,4,192]{0,2,1:T(8,128)(2,1)S(1)}, u32[]{:S(2)}, u32[]{:S(2)}) async-start(bf16[256,4,192]{0,2,1:T(8,128)(2,1)} %bitcast.14), calls=%async_computation.1 | async-start | bytes 786432 | tf_op jit(solution)/shard_map/all_to_all | solution.py:154
  94.6 236.6 %reduce-scatter.22.cloned.1.call-start = ((), (), s32[]{:S(2)}) async-start(), calls=%async_computation.22 | async-start | bytes 884736
  161.4 24.5 %copy-start.1 = (bf16[1024,768]{1,0:T(8,128)(2,1)S(1)}, bf16[1024,768]{1,0:T(8,128)(2,1)}, u32[]{:S(2)}) copy-start(bf16[1024,768]{1,0:T(8,128)(2,1)} %all-gather.14.cloned.1.call-done) | copy-start | bytes 4718596
  164.6 168.8 %reduce-scatter.14.cloned.1.call-start = ((), (), s32[]{:S(2)}) async-start(), calls=%async_computation.18 | async-start | bytes 3932160 | tf_op jit(solution)/shard_map/reduce_scatter | solution.py:223
  195.0 178.8 %reduce-scatter.12.cloned.1.call-start = ((), (), s32[]{:S(2)}) async-start(), calls=%async_computation.17 | async-start | bytes 3932160 | tf_op jit(solution)/shard_map/reduce_scatter | solution.py:222
  245.5 63.1 %copy-start.9 = (bf16[768,576]{1,0:T(8,128)(2,1)S(1)}, bf16[768,576]{1,0:T(8,128)(2,1)}, u32[]{:S(2)}) copy-start(bf16[768,576]{1,0:T(8,128)(2,1)} %copy-done.8) | copy-start | bytes 2654212
  311.8 109.1 %reduce-scatter.10.cloned.1.call-start = ((), (), s32[]{:S(2)}) async-start(), calls=%async_computation.15 | async-start | bytes 1966080 | tf_op jit(solution)/shard_map/reduce_scatter | solution.py:157
  316.8 140.7 %reduce-scatter.18.cloned.1.call-start = ((), (), s32[]{:S(2)}) async-start(), calls=%async_computation.20 | async-start | bytes 2654208 | tf_op jit(solution)/shard_map/reduce_scatter | solution.py:207
  321.7 182.1 %reduce-scatter.20.cloned.1.call-start = ((), (), s32[]{:S(2)}) async-start(), calls=%async_computation.21 | async-start | bytes 2654208 | tf_op jit(solution)/shard_map/reduce_scatter | solution.py:217
  326.1 221.7 %reduce-scatter.16.cloned.1.call-start = ((), (), s32[]{:S(2)}) async-start(), calls=%async_computation.19 | async-start | bytes 2211840 | tf_op jit(solution)/shard_map/reduce_scatter | solution.py:206
  331.0 42.8 %copy-start = (bf16[256,768]{1,0:T(8,128)(2,1)S(1)}, bf16[256,768]{1,0:T(8,128)(2,1)}, u32[]{:S(2)}) copy-start(bf16[256,768]{1,0:T(8,128)(2,1)} %param.16) | copy-start | bytes 1179652
  331.0 42.8 %copy-start.22 = (f32[768]{0:T(1024)S(1)}, f32[768]{0:T(1024)}, u32[]{:S(2)}) copy-start(f32[768]{0:T(1024)} %param.20) | copy-start | bytes 9220
  331.0 42.8 %copy-start.23 = (f32[768]{0:T(1024)S(1)}, f32[768]{0:T(1024)}, u32[]{:S(2)}) copy-start(f32[768]{0:T(1024)} %param.22) | copy-start | bytes 9220
  331.0 42.8 %copy-start.25 = (f32[256]{0:T(256)S(1)}, f32[256]{0:T(256)}, u32[]{:S(2)}) copy-start(f32[256]{0:T(256)} %copy-done.24) | copy-start | bytes 3076
  331.0 42.8 %copy-start.27 = (f32[256]{0:T(256)S(1)}, f32[256]{0:T(256)}, u32[]{:S(2)}) copy-start(f32[256]{0:T(256)} %copy-done.26) | copy-start | bytes 3076
  331.0 44.8 %copy-start.28 = (f32[768]{0:T(1024)S(1)}, f32[768]{0:T(1024)}, u32[]{:S(2)}) copy-start(f32[768]{0:T(1024)} %get-tuple-element.33) | copy-start | bytes 9220
  331.0 89.9 %copy-start.2 = (bf16[256,768]{1,0:T(8,128)(2,1)S(1)}, bf16[256,768]{1,0:T(8,128)(2,1)}, u32[]{:S(2)}) copy-start(bf16[256,768]{1,0:T(8,128)(2,1)} %get-tuple-element.34) | copy-start | bytes 1179652
  331.0 89.9 %copy-start.32 = (f32[768]{0:T(1024)S(1)}, f32[768]{0:T(1024)}, u32[]{:S(2)}) copy-start(f32[768]{0:T(1024)} %param.31) | copy-start | bytes 9220
  331.0 89.9 %copy-start.33 = (f32[768]{0:T(1024)S(1)}, f32[768]{0:T(1024)}, u32[]{:S(2)}) copy-start(f32[768]{0:T(1024)} %param.27) | copy-start | bytes 9220
  419.5 128.9 %copy-start.34 = (f32[768]{0:T(1024)}, f32[768]{0:T(1024)S(1)}, u32[]{:S(2)}) copy-start(f32[768]{0:T(1024)S(1)} %get-tuple-element.96) | copy-start | bytes 9220
  (24 other events, 92.4 us)
Sparse Core Ops, SparseCore 0:
  12.1 39.7 all-gather.5
  53.7 22.7 all-gather.9
  78.7 45.4 all-gather.7
  125.6 35.8 all-gather.13
  163.2 22.7 all-gather.11
  189.6 34.9 reduce-scatter.21
  226.8 79.1 reduce-scatter.13
  311.9 61.8 reduce-scatter.11
  376.0 36.3 reduce-scatter.9
  416.2 41.1 reduce-scatter.17
  461.4 42.3 reduce-scatter.19
  507.6 40.1 reduce-scatter.15
where the time goes:
time: 556 us; the launch traced here: 555 us
  waiting for transfers between devices  296 us (53%)
  blocking collectives  144 us (26%)
  matrix products  61.7 us (11%)
  other arithmetic  17.4 us (3%)
  between operations  15.5 us (3%)
  local copies, waits for them, and re-layouts  12.7 us (2%)
  starting transfers between devices  7.7 us (1%)
    all_to_all x1, blocking collectives, on_device(): lax.all_to_all(grad_mixed, 'col', split_axis=1, concat_axis=0, tiled=True)  61.8 us
    reduce_scatter x1, waiting for transfers between devices, on_device(): lax.psum_scatter(grad_out_w, 'row', scatter_dimension=1, tiled=True)  46.3 us
    reduce_scatter x1, waiting for transfers between devices, on_device(): lax.psum_scatter(grad_qkv_w, 'row', scatter_dimension=0, tiled=True)  44 us
    psum x1, blocking collectives, on_device(): lax.psum((norm_sums[0], norm_sums[1], norm_sums[2], norm_sums[3], jnp.sum...  43.6 us
    reduce_scatter x1, waiting for transfers between devices, on_device(): lax.psum_scatter(back_first_rows, 'col', scatter_dimension=0, tiled=True)  40.4 us
    reduce_scatter x1, waiting for transfers between devices, on_device(): lax.psum_scatter(grad_in_w, 'row', scatter_dimension=0, tiled=True)  33.4 us
    all_gather x1, waiting for transfers between devices, on_device(): grad_rows = lax.all_gather(grad_out, 'col', axis=0, tiled=True)  31.8 us
    all_gather x1, waiting for transfers between devices, on_device(): lax.all_gather(normed_second, 'col', axis=0, tiled=True)  29.5 us
  transfers between devices with their start and end apart: 14, of which 9 were waited for; matrix products, arithmetic and copies ran while one was open for 15% of the time, Pallas kernels for 0%

commit v1 on v0

--- a/solution.py
+++ b/solution.py
@@ -9,6 +9,11 @@
 NORM_EPSILON = 1e-05
 HALF_ROOT = math.sqrt(0.5)
 DENSITY_SCALE = 1.0 / math.sqrt(2.0 * math.pi)
+
+
+def one_after_other(array, axis_one, axis_two):
+    partial = lax.psum(array, axis_one)
+    return lax.psum(partial, axis_two)
 
 
 def normalize(features):
@@ -240,7 +245,7 @@
     in_bias_part = jnp.sum(grad_pre, axis=0, dtype=jnp.float32)
     spread_qkv = jnp.where(column_mask, qkv_bias_part[None, :], 0.0).reshape(-1)
     spread_in = jnp.where(column_mask, in_bias_part[None, :], 0.0).reshape(-1)
-    gain_one, bias_one, gain_two, bias_two, out_bias, total_qkv, total_in = lax.psum(
+    gain_one, bias_one, gain_two, bias_two, out_bias, total_qkv, total_in = one_after_other(
         (
             norm_sums[0],
             norm_sums[1],
@@ -250,7 +255,8 @@
             spread_qkv,
             spread_in,
         ),
-        ("row", "col"),
+        "col",
+        "row",
     )
     qkv_bias_grad = lax.dynamic_slice_in_dim(total_qkv, col_index * qkv_cols, qkv_cols, 0)
     fc_in_bias_grad = lax.dynamic_slice_in_dim(total_in, col_index * ff_cols, ff_cols, 0)

time: 556 us -> 556 us (level)
    psum x1 -> x2, blocking collectives: 43.6 us -> 43 us  [the longest x1 23.8 us: one_after_other(): return lax.psum(partial, axis_two)]
where the time goes in v1:
time: 556 us; the launch traced here: 555 us
  waiting for transfers between devices  297 us (53%)
  blocking collectives  143 us (26%)
  matrix products  61.5 us (11%)
  other arithmetic  17.3 us (3%)
  between operations  15.5 us (3%)
  local copies, waits for them, and re-layouts  12.7 us (2%)
  starting transfers between devices  7.7 us (1%)
    all_to_all x1, blocking collectives, on_device(): lax.all_to_all(grad_mixed, 'col', split_axis=1, concat_axis=0, tiled=True)  61.8 us
    reduce_scatter x1, waiting for transfers between devices, on_device(): lax.psum_scatter(grad_out_w, 'row', scatter_dimension=1, tiled=True)  46.3 us
    reduce_scatter x1, waiting for transfers between devices, on_device(): lax.psum_scatter(grad_qkv_w, 'row', scatter_dimension=0, tiled=True)  44 us
    reduce_scatter x1, waiting for transfers between devices, on_device(): lax.psum_scatter(back_first_rows, 'col', scatter_dimension=0, tiled=True)  40.5 us
    reduce_scatter x1, waiting for transfers between devices, on_device(): lax.psum_scatter(grad_in_w, 'row', scatter_dimension=0, tiled=True)  34 us
    all_gather x1, waiting for transfers between devices, on_device(): grad_rows = lax.all_gather(grad_out, 'col', axis=0, tiled=True)  31.8 us
    all_gather x1, waiting for transfers between devices, on_device(): lax.all_gather(normed_second, 'col', axis=0, tiled=True)  29.5 us
    all_gather x1, waiting for transfers between devices, on_device(): lax.all_gather(normed_first, 'col', axis=0, tiled=True)  23.8 us
  transfers between devices with their start and end apart: 14, of which 9 were waited for; matrix products, arithmetic and copies ran while one was open for 15% of the time, Pallas kernels for 0%

profile of v1, /device:TPU:0, one launch (start us, length us, event | category | flops | bytes accessed | tf_op | source)
XLA Modules:
  0.0 555.1 jit_solution(15045029151046150173)
XLA Ops:
  9.7 2.2 fusion.38
  15.7 12.3 %all_gather.22 = bf16[768,576]{1,0:T(8,128)(2,1)S(1)} all-gather(bf16[96,576]{1,0:T(8,128)(2,1)S(1)} %copy-done.18), channel_id=1, replica_groups=mesh['row'=8,'col'=4] {'row'}, dimensions={0}, use_global_device_ids=true | all-gather | bytes 995328 | tf_op jit(solution)/shard_map/all_gather | solution.py:134
  28.0 23.8 %all-gather.6.cloned.1.call-done = bf16[1024,768]{1,0:T(8,128)(2,1)} async-done(((bf16[256,768]{1,0:T(8,128)(2,1)}), bf16[1024,768]{1,0:T(8,128)(2,1)}) %all-gather.6.cloned.1.call-update) | async-done | bytes 1572880 | tf_op jit(solution)/shard_map/all_gather | solution.py:130
  51.8 2.5 add_convert_fusion.1
  55.5 3.5 all-to-all-start
  63.2 23.8 %all-to-all-done = bf16[4,256,576]{1,2,0:T(8,128)(2,1)S(1)} async-done(((bf16[4,256,576]{1,2,0:T(8,128)(2,1)}), bf16[4,256,576]{1,2,0:T(8,128)(2,1)S(1)}, u32[]{:S(2)}, u32[]{:S(2)}) %all-to-all-start) | async-done | bytes 1179680 | tf_op jit(solution)/shard_map/all_to_all | solution.py:142
  91.2 3.5 all-to-all-start.1
  94.7 29.5 %all-gather.8.cloned.1.call-done = bf16[1024,768]{1,0:T(8,128)(2,1)} async-done(((bf16[256,768]{1,0:T(8,128)(2,1)}), bf16[1024,768]{1,0:T(8,128)(2,1)}) %all-gather.8.cloned.1.call-update) | async-done | bytes 1572880 | tf_op jit(solution)/shard_map/all_gather | solution.py:131
  124.2 5.4 multiply_convert_fusion.1
  129.6 31.8 %all-gather.14.cloned.1.call-done = bf16[1024,768]{1,0:T(8,128)(2,1)} async-done(((bf16[256,768]{1,0:T(8,128)(2,1)}), bf16[1024,768]{1,0:T(8,128)(2,1)}) %all-gather.14.cloned.1.call-update) | async-done | bytes 1572880 | tf_op jit(solution)/shard_map/all_gather | solution.py:173
  161.4 3.1 convolution_bitcast_fusion
  164.6 21.3 %all-gather.12.cloned.1.call-done = bf16[768,768]{0,1:T(8,128)(2,1)} async-done(((bf16[768,96]{0,1:T(8,128)(2,1)}), bf16[768,768]{0,1:T(8,128)(2,1)}) %all-gather.12.cloned.1.call-update) | async-done | bytes 1179664 | tf_op jit(solution)/shard_map/all_gather | solution.py:137
  186.0 4.7 convert_reduce_fusion
  191.9 3.1 fusion.99
  196.5 9.5 %all_gather.23 = bf16[192,768]{0,1:T(8,128)(2,1)S(1)} all-gather(bf16[192,96]{0,1:T(8,128)(2,1)} %copy.47), channel_id=1, replica_groups=mesh['row'=8,'col'=4] {'row'}, dimensions={1}, use_global_device_ids=true | all-gather | bytes 331776 | tf_op jit(solution)/shard_map/all_gather | solution.py:136
  206.7 16.6 %all_to_all.70 = bf16[4,256,192]{1,2,0:T(8,128)(2,1)S(1)} all-to-all(bf16[4,256,192]{1,2,0:T(8,128)(2,1)S(1)} %bitcast.111), channel_id=1, replica_groups=mesh['row'=8,'col'=4] {'col'}, dimensions={0} | all-to-all | bytes 786432 | tf_op jit(solution)/shard_map/all_to_all | solution.py:179
  224.1 2.3 fusion.53
  226.4 6.9 %fusion.19 = f32[256,12,64]{0,2,1:T(8,128)S(1)} fusion(f32[12,256,256]{1,2,0:T(8,128)} %fusion.53, f32[12,256,256]{1,2,0:T(8,128)} %copy-done.3, f32[12,256]{1,0:T(8,128)} %copy-done.29, pred[256,256]{0,1:T(8,128)(4,1)} %copy-done.14, bf16[256,12,48]{0,2,1:T(8,128)(2,1)} %copy-done.11, bf16[256,12,16]{0,2,1:T(8,128)(2,1)} %copy-done.20), kind=kOutput, calls=%fused_computation.25 | convolution fusion | flops 110103808 | bytes 7548928 | tf_op jit(solution)/shard_map/phij,pjhd->pihd/dot_general | solution.py:186
  233.4 7.8 %fusion.22 = f32[256,12,64]{0,2,1:T(8,128)} fusion(f32[12,256,256]{1,2,0:T(8,128)} %fusion.53, f32[12,256,256]{1,2,0:T(8,128)} %copy-done.3, f32[12,256]{1,0:T(8,128)S(1)} %copy-done.30, pred[256,256]{0,1:T(8,128)(4,1)} %copy-done.14, bf16[256,12,48]{0,2,1:T(8,128)(2,1)S(1)} %copy-done.13, bf16[256,12,16]{0,2,1:T(8,128)(2,1)} %copy-done.19), kind=kOutput, calls=%fused_computation.26 | convolution fusion | flops 110103808 | bytes 7548928 | tf_op jit(solution)/shard_map/phij,pihd->pjhd/dot_general | solution.py:189
  245.5 61.8 %all_to_all.71 = bf16[256,4,576]{0,2,1:T(8,128)(2,1)S(1)} all-to-all(bf16[256,4,576]{0,2,1:T(8,128)(2,1)S(1)} %bitcast.104), channel_id=1, replica_groups=mesh['row'=8,'col'=4] {'col'}, dimensions={1} | all-to-all | bytes 2359296 | tf_op jit(solution)/shard_map/all_to_all | solution.py:203
  308.5 3.1 fusion.98
  311.7 3.2 fusion.97
  316.8 4.8 fusion.101
  321.6 4.3 fusion.102
  326.3 4.6 fusion.100
  333.3 40.5 %reduce-scatter.12.cloned.1.call-done = f32[256,768]{1,0:T(8,128)} async-done(((f32[1024,768]{1,0:T(8,128)}), f32[256,768]{1,0:T(8,128)}) %reduce-scatter.12.cloned.1.call-update) | async-done | bytes 786448 | tf_op jit(solution)/shard_map/reduce_scatter | solution.py:227
  375.9 19.2 %all-reduce.1 = (f32[768]{0:T(1024)S(1)}, f32[768]{0:T(1024)S(1)}, f32[768]{0:T(1024)S(1)}, f32[768]{0:T(1024)S(1)}, f32[2304]{0:T(1024)S(1)}, /*index=5*/f32[768]{0:T(1024)S(1)}, f32[3072]{0:T(1024)S(1)}) all-reduce(f32[768]{0:T(1024)S(1)} %get-tuple-element.16, ...), channel_id=1, replica_groups=mesh['row'=8,'col'=4] {'col'}, use_global_device_ids=true, to_apply=%region_13.14 | all-reduce | flops 9216 | bytes 73728 | tf_op jit(solution)/shard_map/psum | solution.py:15
  395.1 23.8 %all-reduce = (f32[768]{0:T(1024)}, f32[768]{0:T(1024)}, f32[768]{0:T(1024)}, f32[768]{0:T(1024)}, f32[2304]{0:T(1024)S(1)}, /*index=5*/f32[768]{0:T(1024)S(1)}, f32[3072]{0:T(1024)S(1)}) all-reduce(f32[768]{0:T(1024)S(1)} %get-tuple-element.33, f32[768]{0:T(1024)S(1)} %get-tuple-element.34, ...), channel_id=1, replica_groups=mesh['row'=8,'col'=4] {'row'}, use_global_device_ids=true, to_apply=%region_14.15 | all-reduce | flops 9216 | bytes 73728 | tf_op jit(solution)/shard_map/psum | solution.py:16
  420.3 3.1 fusion.47
  423.4 34.0 %reduce-scatter.18.cloned.1.call-done = f32[96,768]{1,0:T(8,128)} async-done(((f32[768,768]{1,0:T(8,128)}), f32[96,768]{1,0:T(8,128)}) %reduce-scatter.18.cloned.1.call-update) | async-done | bytes 294928 | tf_op jit(solution)/shard_map/reduce_scatter | solution.py:212
  457.4 46.3 %reduce-scatter.20.cloned.1.call-done = f32[768,96]{0,1:T(8,128)} async-done(((f32[768,768]{0,1:T(8,128)}), f32[768,96]{0,1:T(8,128)}) %reduce-scatter.20.cloned.1.call-update) | async-done | bytes 294928 | tf_op jit(solution)/shard_map/reduce_scatter | solution.py:222
  503.7 44.0 %reduce-scatter.16.cloned.1.call-done = f32[96,576]{1,0:T(8,128)} async-done(((f32[768,576]{1,0:T(8,128)}), f32[96,576]{1,0:T(8,128)}) %reduce-scatter.16.cloned.1.call-update) | async-done | bytes 221200 | tf_op jit(solution)/shard_map/reduce_scatter | solution.py:211
  (167 shorter events, 33.2 us)
Async XLA Ops:
  7.2 8.5 %copy-start.18 = (bf16[96,576]{1,0:T(8,128)(2,1)S(1)}, bf16[96,576]{1,0:T(8,128)(2,1)}, u32[]{:S(2)}) copy-start(bf16[96,576]{1,0:T(8,128)(2,1)} %param.24) | copy-start | bytes 331780
  7.2 44.6 %copy-start.38 = (f32[576]{0:T(1024)S(1)}, f32[576]{0:T(1024)}, u32[]{:S(2)}) copy-start(f32[576]{0:T(1024)} %param.25) | copy-start | bytes 6916
  7.2 44.6 %all-gather.6.cloned.1.call-start = ((), (), s32[]{:S(2)}) async-start(), calls=%async_computation.11 | async-start | bytes 1966080 | tf_op jit(solution)/shard_map/all_gather | solution.py:130
  11.9 82.8 %all-gather.10.cloned.1.call-start = ((), (), s32[]{:S(2)}) async-start(), calls=%async_computation.13 | async-start | bytes 1327104 | tf_op jit(solution)/shard_map/all_gather | solution.py:135
  12.7 111.5 %all-gather.8.cloned.1.call-start = ((), (), s32[]{:S(2)}) async-start(), calls=%async_computation.12 | async-start | bytes 1966080 | tf_op jit(solution)/shard_map/all_gather | solution.py:131
  13.4 148.0 %all-gather.14.cloned.1.call-start = ((), (), s32[]{:S(2)}) async-start(), calls=%async_computation.16 | async-start | bytes 1966080 | tf_op jit(solution)/shard_map/all_gather | solution.py:173
  28.0 26.4 %copy-start.8 = (bf16[768,576]{1,0:T(8,128)(2,1)}, bf16[768,576]{1,0:T(8,128)(2,1)S(1)}, u32[]{:S(2)}) copy-start(bf16[768,576]{1,0:T(8,128)(2,1)S(1)} %all_gather.22) | copy-start | bytes 2654212
  55.5 31.4 %all-to-all-start = ((bf16[4,256,576]{1,2,0:T(8,128)(2,1)}), bf16[4,256,576]{1,2,0:T(8,128)(2,1)S(1)}, u32[]{:S(2)}, u32[]{:S(2)}) async-start(bf16[4,256,576]{1,2,0:T(8,128)(2,1)} %bitcast.101), calls=%async_computation | async-start | bytes 2359296 | tf_op jit(solution)/shard_map/all_to_all | solution.py:142
  59.1 126.9 %all-gather.12.cloned.1.call-start = ((), (), s32[]{:S(2)}) async-start(), calls=%async_computation.14 | async-start | bytes 1327104 | tf_op jit(solution)/shard_map/all_gather | solution.py:137
  63.0 25.8 %copy-start.16 = (f32[256,16]{0,1:T(8,128)}, f32[256,16]{0,1:T(8,128)S(1)}, u32[]{:S(2)}) copy-start(f32[256,16]{0,1:T(8,128)S(1)} %get-tuple-element.65) | copy-start | bytes 49156
  63.2 26.4 %copy-start.14 = (pred[256,256]{0,1:T(8,128)(4,1)}, pred[256,256]{0,1:T(8,128)(4,1)S(1)}, u32[]{:S(2)}) copy-start(pred[256,256]{0,1:T(8,128)(4,1)S(1)} %fusion.57) | copy-start | bytes 196612
  89.5 34.7 %copy-start.39 = (f32[768]{0:T(1024)S(1)}, f32[768]{0:T(1024)}, u32[]{:S(2)}) copy-start(f32[768]{0:T(1024)} %param.29) | copy-start | bytes 9220
  91.2 38.4 %all-to-all-start.1 = ((bf16[256,4,192]{0,2,1:T(8,128)(2,1)}), bf16[256,4,192]{0,2,1:T(8,128)(2,1)S(1)}, u32[]{:S(2)}, u32[]{:S(2)}) async-start(bf16[256,4,192]{0,2,1:T(8,128)(2,1)} %bitcast.14), calls=%async_computation.1 | async-start | bytes 786432 | tf_op jit(solution)/shard_map/all_to_all | solution.py:159
  94.6 236.5 %reduce-scatter.22.cloned.1.call-start = ((), (), s32[]{:S(2)}) async-start(), calls=%async_computation.22 | async-start | bytes 884736
  161.4 24.5 %copy-start.1 = (bf16[1024,768]{1,0:T(8,128)(2,1)S(1)}, bf16[1024,768]{1,0:T(8,128)(2,1)}, u32[]{:S(2)}) copy-start(bf16[1024,768]{1,0:T(8,128)(2,1)} %all-gather.14.cloned.1.call-done) | copy-start | bytes 4718596
  164.6 168.7 %reduce-scatter.14.cloned.1.call-start = ((), (), s32[]{:S(2)}) async-start(), calls=%async_computation.18 | async-start | bytes 3932160 | tf_op jit(solution)/shard_map/reduce_scatter | solution.py:228
  195.0 178.8 %reduce-scatter.12.cloned.1.call-start = ((), (), s32[]{:S(2)}) async-start(), calls=%async_computation.17 | async-start | bytes 3932160 | tf_op jit(solution)/shard_map/reduce_scatter | solution.py:227
  245.4 63.1 %copy-start.9 = (bf16[768,576]{1,0:T(8,128)(2,1)S(1)}, bf16[768,576]{1,0:T(8,128)(2,1)}, u32[]{:S(2)}) copy-start(bf16[768,576]{1,0:T(8,128)(2,1)} %copy-done.8) | copy-start | bytes 2654212
  311.7 108.5 %reduce-scatter.10.cloned.1.call-start = ((), (), s32[]{:S(2)}) async-start(), calls=%async_computation.15 | async-start | bytes 1966080 | tf_op jit(solution)/shard_map/reduce_scatter | solution.py:162
  316.7 140.6 %reduce-scatter.18.cloned.1.call-start = ((), (), s32[]{:S(2)}) async-start(), calls=%async_computation.20 | async-start | bytes 2654208 | tf_op jit(solution)/shard_map/reduce_scatter | solution.py:212
  321.6 182.1 %reduce-scatter.20.cloned.1.call-start = ((), (), s32[]{:S(2)}) async-start(), calls=%async_computation.21 | async-start | bytes 2654208 | tf_op jit(solution)/shard_map/reduce_scatter | solution.py:222
  326.0 221.7 %reduce-scatter.16.cloned.1.call-start = ((), (), s32[]{:S(2)}) async-start(), calls=%async_computation.19 | async-start | bytes 2211840 | tf_op jit(solution)/shard_map/reduce_scatter | solution.py:211
  330.9 42.9 %copy-start = (bf16[256,768]{1,0:T(8,128)(2,1)S(1)}, bf16[256,768]{1,0:T(8,128)(2,1)}, u32[]{:S(2)}) copy-start(bf16[256,768]{1,0:T(8,128)(2,1)} %param.16) | copy-start | bytes 1179652
  330.9 42.9 %copy-start.22 = (f32[768]{0:T(1024)S(1)}, f32[768]{0:T(1024)}, u32[]{:S(2)}) copy-start(f32[768]{0:T(1024)} %param.20) | copy-start | bytes 9220
  330.9 42.9 %copy-start.23 = (f32[768]{0:T(1024)S(1)}, f32[768]{0:T(1024)}, u32[]{:S(2)}) copy-start(f32[768]{0:T(1024)} %param.22) | copy-start | bytes 9220
  330.9 42.9 %copy-start.25 = (f32[256]{0:T(256)S(1)}, f32[256]{0:T(256)}, u32[]{:S(2)}) copy-start(f32[256]{0:T(256)} %copy-done.24) | copy-start | bytes 3076
  330.9 42.9 %copy-start.27 = (f32[256]{0:T(256)S(1)}, f32[256]{0:T(256)}, u32[]{:S(2)}) copy-start(f32[256]{0:T(256)} %copy-done.26) | copy-start | bytes 3076
  330.9 45.0 %copy-start.28 = (f32[768]{0:T(1024)S(1)}, f32[768]{0:T(1024)}, u32[]{:S(2)}) copy-start(f32[768]{0:T(1024)} %get-tuple-element.40) | copy-start | bytes 9220
  330.9 89.3 %copy-start.2 = (bf16[256,768]{1,0:T(8,128)(2,1)S(1)}, bf16[256,768]{1,0:T(8,128)(2,1)}, u32[]{:S(2)}) copy-start(bf16[256,768]{1,0:T(8,128)(2,1)} %get-tuple-element.41) | copy-start | bytes 1179652
  330.9 89.3 %copy-start.32 = (f32[768]{0:T(1024)S(1)}, f32[768]{0:T(1024)}, u32[]{:S(2)}) copy-start(f32[768]{0:T(1024)} %param.31) | copy-start | bytes 9220
  330.9 89.3 %copy-start.33 = (f32[768]{0:T(1024)S(1)}, f32[768]{0:T(1024)}, u32[]{:S(2)}) copy-start(f32[768]{0:T(1024)} %param.27) | copy-start | bytes 9220
  418.9 129.4 %copy-start.34 = (f32[768]{0:T(1024)}, f32[768]{0:T(1024)S(1)}, u32[]{:S(2)}) copy-start(f32[768]{0:T(1024)S(1)} %get-tuple-element.103) | copy-start | bytes 9220
  (24 other events, 92.3 us)
Sparse Core Ops, SparseCore 0:
  12.1 39.7 all-gather.5
  53.7 22.7 all-gather.9
  78.7 45.4 all-gather.7
  125.6 35.8 all-gather.13
  163.2 22.7 all-gather.11
  189.6 34.9 reduce-scatter.21
  226.9 79.1 reduce-scatter.13
  311.8 61.8 reduce-scatter.11
  376.1 36.0 reduce-scatter.9
  415.9 41.4 reduce-scatter.17
  461.3 42.3 reduce-scatter.19
  507.5 40.1 reduce-scatter.15
